TPU v7x, 32 devices: a whole 2x2x4 slice. The times are simulated.
32 devices in a mesh: rows: 8 (over z, y), grp: 4 (over x, core).
Axes of the slice: x: 2, y: 2, z: 4, core: 2. Of those that a mesh axis runs over, the one named last changes fastest.
Arguments:
- mat: float32 [16384, 1024], P(('rows', 'grp'))
- signs: int32 [16384], P(('rows', 'grp')), may hold values from -1 to 1, as said below
- picks: int32 [2048], P(('rows', 'grp')), may hold values from 0 to 16383, as said below
- rhs: float32 [16384, 128], P(('rows', 'grp'))
Outputs:
- tri: float32 [1024, 1024], replicated
- solution: float32 [1024, 128], replicated
- residual: float32 [16384, 128], P(('rows', 'grp'))
Inputs may be any that keep to these rules, and one draw needn't show every extreme that they name: `signs`: every entry is -1 or 1. `picks`: the entries k * 64 to (k + 1) * 64 - 1 are distinct row indices in k * 512 to (k + 1) * 512 - 1.
All inputs are finite; a program needn't handle non-finite values.
Results may differ from a plain program's by a relative error of at most 0.000088.
Values sent between devices are 32-bit elements; how exact they have to be, the bound alone decides.
A program may use at most 64 MiB of HBM per device.

v0:
```python
import functools

import jax
import jax.numpy as jnp
from jax import lax
from jax.experimental import pallas as pl
from jax.experimental.pallas import tpu as pltpu
from jax.sharding import PartitionSpec as P

exact_mode = lax.Precision.HIGHEST
TILE = 128
SUB = 8
AXES = ("rows", "grp")


def walsh_table(table_order, piece=1):
    counter = lax.iota(jnp.int32, table_order)
    outer = counter // piece
    common_bits = outer[:, None] & outer[None, :]
    parity = jnp.zeros((table_order, table_order), jnp.int32)
    for bit_pos in range(max((table_order // piece).bit_length() - 1, 0)):
        parity = parity + (common_bits >> bit_pos & 1)
    table = jnp.where(parity % 2 == 0, 1.0, -1.0).astype(jnp.float32)
    inner = counter % piece
    return jnp.where(inner[:, None] == inner[None, :], table, 0.0)


def dot_tt(a, b):
    return lax.dot_general(a, b, (((0,), (0,)), ((), ())), precision=exact_mode,
                           preferred_element_type=jnp.float32)


def dot_nn(a, b):
    return lax.dot_general(a, b, (((1,), (0,)), ((), ())), precision=exact_mode,
                           preferred_element_type=jnp.float32)


def factor_tile(block):
    groups = TILE // SUB
    lane = lax.broadcasted_iota(jnp.int32, (SUB, TILE), 1)
    sub = lax.broadcasted_iota(jnp.int32, (SUB, TILE), 0)
    left = [block[SUB * g:SUB * (g + 1), :] for g in range(groups)]
    right = [(lane == sub + SUB * g).astype(jnp.float32) for g in range(groups)]
    for j in range(TILE):
        g, s = divmod(j, SUB)
        inv = 1.0 / left[g][s:s + 1, j:j + 1]
        row = left[g][s:s + 1, :] * inv
        row_e = right[g][s:s + 1, :] * inv
        for h in range(g, groups):
            col = jnp.broadcast_to(left[h][:, j:j + 1], (SUB, TILE))
            if h == g:
                if s == SUB - 1:
                    continue
                col = jnp.where(sub > s, col, 0.0)
            left[h] = left[h] - col * row
            right[h] = right[h] - col * row_e
    for g in range(groups):
        pivot = jnp.sum(jnp.where(lane == sub + SUB * g, left[g], 0.0), axis=1, keepdims=True)
        root = jnp.sqrt(pivot)
        left[g] = jnp.where(lane >= sub + SUB * g, left[g] / root, 0.0)
        right[g] = jnp.where(lane <= sub + SUB * g, right[g] / root, 0.0)
    return jnp.concatenate(left, axis=0), jnp.concatenate(right, axis=0)


def factor_kernel(packed_ref, atb_ref, squares_ref, tri_ref, direction_ref, alpha_ref, work, inverse):
    n = tri_ref.shape[0]
    tiles = n // TILE
    offset = 0
    for i in range(tiles):
        for j in range(i, tiles):
            work[i * TILE:(i + 1) * TILE, j * TILE:(j + 1) * TILE] = packed_ref[offset:offset + TILE, :]
            offset += TILE
        if i:
            work[i * TILE:(i + 1) * TILE, :i * TILE] = jnp.zeros((TILE, i * TILE), jnp.float32)
    work[:, n:] = atb_ref[...]
    width = work.shape[1]

    def step(k, carry):
        at = pl.multiple_of(k * TILE, TILE)
        here = pl.ds(at, TILE)
        upper, inv = factor_tile(work[here, here])
        inverse[here, :] = inv
        column = lax.broadcasted_iota(jnp.int32, (TILE, width), 1)
        panel = dot_nn(inv, work[here, :])
        work[here, :] = jnp.where(column >= at + TILE, panel, 0.0)
        work[here, here] = upper

        def trail(i, carry):
            there = pl.ds(pl.multiple_of(i * TILE, TILE), TILE)
            work[there, :] = work[there, :] - dot_tt(work[here, there], work[here, :])
            return carry

        return lax.fori_loop(k + 1, tiles, trail, carry)

    lax.fori_loop(0, tiles, step, 0)
    tri_ref[...] = work[:, :n]
    beta = jnp.sqrt(squares_ref[0:1, :])
    lifted = work[:, n:] / beta
    alpha = jnp.sqrt(jnp.sum(lifted * lifted, axis=0, keepdims=True))
    alpha_ref[...] = jnp.broadcast_to(alpha, alpha_ref.shape)
    work[:, n:] = lifted / alpha
    direction_ref[...] = jnp.zeros_like(direction_ref)

    def back(t, carry):
        k = tiles - 1 - t
        here = pl.ds(pl.multiple_of(k * TILE, TILE), TILE)
        rest = work[here, n:] - dot_nn(tri_ref[here, :], direction_ref[...])
        direction_ref[here, :] = dot_tt(inverse[here, :], rest)
        return carry

    lax.fori_loop(0, tiles, back, 0)


def factor_and_solve(packed, atb, squares):
    n, k = atb.shape
    return pl.pallas_call(
        factor_kernel,
        out_shape=(
            jax.ShapeDtypeStruct((n, n), jnp.float32),
            jax.ShapeDtypeStruct((n, k), jnp.float32),
            jax.ShapeDtypeStruct((SUB, k), jnp.float32),
        ),
        in_specs=[pl.BlockSpec(memory_space=pltpu.VMEM)] * 3,
        out_specs=(pl.BlockSpec(memory_space=pltpu.VMEM),) * 3,
        scratch_shapes=[
            pltpu.VMEM((n, n + k), jnp.float32),
            pltpu.VMEM((n, TILE), jnp.float32),
        ],
        compiler_params=pltpu.CompilerParams(vmem_limit_bytes=48 * 1024 * 1024),
        name="factor_and_solve",
    )(packed, atb, squares)


def shards(mat, signs, picks, rhs):
    row_count, n = mat.shape
    devices = lax.axis_size("rows") * lax.axis_size("grp")
    samples = picks.shape[0] * devices
    piece = row_count // devices

    atb_part = dot_tt(mat, rhs)
    atb = lax.psum(atb_part, AXES)

    local_rows = lax.iota(jnp.int32, row_count)
    hits = jnp.sum(
        ((picks % row_count)[:, None] == local_rows[None, :]).astype(jnp.float32), axis=0
    ) * (1.0 / samples)
    squares_part = jnp.sum(rhs * rhs, axis=0, keepdims=True)
    small = jnp.concatenate(
        [
            jnp.broadcast_to(squares_part, (devices, rhs.shape[1])),
            hits.reshape(devices, piece),
        ],
        axis=1,
    )
    small = lax.all_to_all(small, AXES, 0, 0, tiled=True)
    hits = small[:, rhs.shape[1]:]
    squares = jnp.broadcast_to(
        jnp.sum(small[:, :rhs.shape[1]], axis=0, keepdims=True), (SUB, rhs.shape[1])
    )

    mixed = mat * signs.astype(jnp.float32)[:, None]
    mixed = dot_nn(walsh_table(row_count), mixed)
    if piece % SUB == 0:
        turned = lax.all_to_all(mixed, AXES, 0, 0, tiled=True)
    else:
        turned = mixed.reshape(devices, piece * n // TILE, TILE)
        turned = lax.all_to_all(turned, AXES, 0, 0, tiled=True).reshape(row_count, n)
    turned = dot_nn(walsh_table(row_count, piece), turned)
    weighted = turned * hits.reshape(row_count, 1)
    strips = [
        dot_tt(weighted[:, at:at + TILE], turned[:, at:]) for at in range(0, n, TILE)
    ]
    tiles = [
        strip[:, at:at + TILE] for strip in strips for at in range(0, strip.shape[1], TILE)
    ]
    packed = lax.psum(jnp.concatenate(tiles, axis=0), AXES)

    tri, direction, alpha = factor_and_solve(packed, atb, squares)
    alpha = alpha[0]
    beta = jnp.sqrt(squares[0])
    image = dot_nn(mat, direction)
    pushed = image - alpha / beta * rhs
    gamma_part = jnp.sum(pushed * pushed, axis=0, keepdims=True)
    gamma_parts = lax.all_to_all(
        jnp.broadcast_to(gamma_part, (devices, rhs.shape[1])), AXES, 0, 0, tiled=True
    )
    gamma_sq = jnp.sum(gamma_parts, axis=0)
    coef = beta * alpha / (alpha * alpha + gamma_sq)
    return (tri, direction * coef, rhs - image * coef)


def solution(mesh):
    return jax.shard_map(
        shards,
        mesh=mesh,
        in_specs=(P(AXES, None), P(AXES), P(AXES), P(AXES, None)),
        out_specs=(P(), P(), P(AXES, None)),
        check_vma=False,
    )
```

profile of v0, /device:TPU:0, one launch (start us, length us, event | category | flops | bytes accessed | tf_op | source)
XLA Modules:
  0.0 396.7 jit_solution(1145848020217883029)
XLA Ops:
  7.2 0.7 and_select_fusion
  8.0 1.0 multiply_reduce_fusion.1
  9.1 0.6 all_to_all.23
  9.7 7.3 %all-to-all-start.1 = ((f32[32,1,144]{2,1,0:T(1,128)}), f32[32,1,144]{2,1,0:T(1,128)S(1)}, u32[]{:S(2)}, u32[]{:S(2)}) async-start(f32[32,1,144]{2,1,0:T(1,128)} %all_to_all.23), calls=%async_computation.1 | async-start | bytes 65536 | tf_op jit(solution)/shard_map/all_to_all | solution.py:155
  17.0 0.7 convert_element_type.6
  17.7 7.8 %fusion = f32[512,1024]{1,0:T(8,128)} fusion(f32[512,1024]{1,0:T(8,128)} %param.4, f32[512]{0:T(512)S(1)} %convert_element_type.6), kind=kOutput, calls=%fused_computation.5 | convolution fusion | flops 3232235520 | bytes 4196352 | tf_op jit(solution)/shard_map/dot_general | solution.py:34
  25.5 6.0 %all-to-all-start = ((f32[32,16,1024]{2,1,0:T(8,128)}), f32[32,16,1024]{2,1,0:T(8,128)}, u32[]{:S(2)}, u32[]{:S(2)}) async-start(f32[32,16,1024]{2,1,0:T(8,128)} %bitcast.34), calls=%async_computation | async-start | bytes 4194304 | tf_op jit(solution)/shard_map/all_to_all | solution.py:164
  31.8 4.2 %fusion.102 = f32[1024,128]{1,0:T(8,128)} fusion(f32[512,1024]{1,0:T(8,128)S(1)} %copy-done.2, f32[512,128]{1,0:T(8,128)S(1)} %copy-done.3), kind=kOutput, calls=%fused_computation.170 | convolution fusion | flops 805306368 | bytes 2883584 | tf_op jit(solution)/shard_map/dot_general | solution.py:29
  36.1 44.1 %all-to-all-done = f32[32,16,1024]{2,1,0:T(8,128)} async-done(((f32[32,16,1024]{2,1,0:T(8,128)}), f32[32,16,1024]{2,1,0:T(8,128)}, u32[]{:S(2)}, u32[]{:S(2)}) %all-to-all-start) | async-done | bytes 2097184 | tf_op jit(solution)/shard_map/all_to_all | solution.py:164
  80.2 6.1 %broadcast_multiply_fusion = (f32[512,1024]{1,0:T(8,128)S(1)}, f32[512,1024]{1,0:T(8,128)S(1)}) fusion(f32[512]{0:T(512)S(1)} %mul.76, f32[512,1024]{1,0:T(8,128)} %bitcast.1, s32[512]{0:T(512)S(1)} %get-tuple-element.30, s32[512]{0:T(512)S(1)} %get-tuple-element.31), kind=kOutput, calls=%fused_computation.36 | convolution fusion | flops 3229614080 | bytes 6297600 | tf_op jit(solution)/shard_map/dot_general | solution.py:34
  86.4 1.3 fusion.72
  87.7 1.2 fusion.2
  88.9 1.1 fusion.4
  90.0 1.0 fusion.6
  91.0 1.0 fusion.21
  92.0 0.7 fusion.37
  93.4 0.6 constant_dynamic-update-slice_fusion.34
  94.0 0.6 constant_dynamic-update-slice_fusion.33
  95.3 0.6 constant_dynamic-update-slice_fusion.31
  95.9 0.6 constant_dynamic-update-slice_fusion.30
  96.6 0.6 constant_dynamic-update-slice_fusion.29
  97.2 0.6 constant_dynamic-update-slice_fusion.28
  97.9 0.6 constant_dynamic-update-slice_fusion.27
  115.6 1.2 convolution_dynamic-update-slice_fusion
  117.1 137.1 %all-reduce.3.cloned.1.call-done = (f32[4608,128]{1,0:T(8,128)}, f32[1024,128]{1,0:T(8,128)}) async-done(((f32[4608,128]{1,0:T(8,128)}, f32[1024,128]{1,0:T(8,128)}), (f32[4608,128]{1,0:T(8,128)}, f32[1024,128]{1,0:T(8,128)})) %all-reduce.3.cloned.1.call-update) | async-done | bytes 2883600 | tf_op jit(solution)/shard_map/psum | solution.py:176
  254.2 1.7 copy-done
  255.8 1.0 copy-done.1
  256.9 118.8 %factor_and_solve.1 = (f32[1024,1024]{1,0:T(8,128)}, f32[1024,128]{1,0:T(8,128)S(1)}, f32[8,128]{1,0:T(8,128)S(1)}) custom-call(f32[4608,128]{1,0:T(8,128)S(1)} %copy-done, f32[1024,128]{1,0:T(8,128)S(1)} %copy-done.1, f32[8,128]{1,0:T(8,128)S(1)} %broadcast_in_dim.25.squares_ref), custom_call_target="tpu_custom_call" | custom-call | tf_op jit(solution)/shard_map/factor_and_solve/pallas_call | solution.py:116
  375.7 2.0 multiply_reduce_fusion
  377.7 10.4 %all_to_all.30 = f32[32,1,128]{2,1,0:T(1,128)S(1)} all-to-all(f32[32,1,128]{2,1,0:T(1,128)S(1)} %broadcast_in_dim.26), channel_id=1, replica_groups=mesh['rows'=8,'grp'=4] {'rows','grp'}, dimensions={0} | all-to-all | bytes 32768 | tf_op jit(solution)/shard_map/all_to_all | solution.py:184
  388.1 0.8 broadcast_multiply_fusion.1
  389.0 0.8 copy.22
  (55 shorter events, 19.2 us)
Async XLA Ops:
  9.7 15.8 %all-to-all-start.1 = ((f32[32,1,144]{2,1,0:T(1,128)}), f32[32,1,144]{2,1,0:T(1,128)S(1)}, u32[]{:S(2)}, u32[]{:S(2)}) async-start(f32[32,1,144]{2,1,0:T(1,128)} %all_to_all.23), calls=%async_computation.1 | async-start | bytes 65536 | tf_op jit(solution)/shard_map/all_to_all | solution.py:155
  25.5 6.2 %copy-start.2 = (f32[512,1024]{1,0:T(8,128)S(1)}, f32[512,1024]{1,0:T(8,128)}, u32[]{:S(2)}) copy-start(f32[512,1024]{1,0:T(8,128)} %param.4) | copy-start | bytes 6291460
  25.5 6.2 %copy-start.3 = (f32[512,128]{1,0:T(8,128)S(1)}, f32[512,128]{1,0:T(8,128)}, u32[]{:S(2)}) copy-start(f32[512,128]{1,0:T(8,128)} %param.7) | copy-start | bytes 786436
  25.5 54.7 %all-to-all-start = ((f32[32,16,1024]{2,1,0:T(8,128)}), f32[32,16,1024]{2,1,0:T(8,128)}, u32[]{:S(2)}, u32[]{:S(2)}) async-start(f32[32,16,1024]{2,1,0:T(8,128)} %bitcast.34), calls=%async_computation | async-start | bytes 4194304 | tf_op jit(solution)/shard_map/all_to_all | solution.py:164
  31.5 222.7 %all-reduce.3.cloned.1.call-start = ((), (), s32[]{:S(2)}) async-start(), calls=%async_computation.3 | async-start | bytes 5767168 | tf_op jit(solution)/shard_map/psum | solution.py:176
  254.2 1.7 copy-start
  255.8 1.0 copy-start.1
Sparse Core Ops, SparseCore 0:
  117.0 137.1 all-reduce.2
where the time goes:
time: 397 us
  waiting for transfers between devices  181 us (46%)
  Pallas kernels  119 us (30%)
  matrix products  28.3 us (7%)
  local copies, waits for them, and re-layouts  26.7 us (7%)
  between operations  14.2 us (4%)
  starting transfers between devices  13.5 us (3%)
  blocking collectives  10.4 us (3%)
    psum x1, waiting for transfers between devices, shards(): packed = lax.psum(jnp.concatenate(tiles, axis=0), AXES)  137 us
    pallas_call x1, Pallas kernels, factor_and_solve(): pl.pallas_call(factor_kernel, out_shape=(jax.ShapeDtypeStruct((n, n), jnp...  119 us
    all_to_all x1, waiting for transfers between devices, shards(): turned = lax.all_to_all(mixed, AXES, 0, 0, tiled=True)  44.1 us
    unnamed x46, local copies, waits for them, and re-layouts  25.9 us
    dot_general x3, matrix products, dot_nn(): lax.dot_general(a, b, (((1,), (0,)), ((), ())), precision=exact_mode, pre...  15.9 us
    dot_general x9, matrix products, dot_tt(): lax.dot_general(a, b, (((0,), (0,)), ((), ())), precision=exact_mode, pre...  12.4 us
    all_to_all x1, blocking collectives, shards(): lax.all_to_all(jnp.broadcast_to(gamma_part, (devices, rhs.shape[1])), AXE...  10.4 us
  transfers between devices with their start and end apart: 3, of which 2 were waited for; matrix products, arithmetic and copies ran while one was open for 3% of the time, Pallas kernels for 0%

commit v1 on v0

--- a/solution.py
+++ b/solution.py
@@ -39,21 +39,35 @@
     groups = TILE // SUB
     lane = lax.broadcasted_iota(jnp.int32, (SUB, TILE), 1)
     sub = lax.broadcasted_iota(jnp.int32, (SUB, TILE), 0)
+    wide = (SUB, TILE)
     left = [block[SUB * g:SUB * (g + 1), :] for g in range(groups)]
     right = [(lane == sub + SUB * g).astype(jnp.float32) for g in range(groups)]
-    for j in range(TILE):
-        g, s = divmod(j, SUB)
-        inv = 1.0 / left[g][s:s + 1, j:j + 1]
-        row = left[g][s:s + 1, :] * inv
-        row_e = right[g][s:s + 1, :] * inv
-        for h in range(g, groups):
-            col = jnp.broadcast_to(left[h][:, j:j + 1], (SUB, TILE))
-            if h == g:
-                if s == SUB - 1:
-                    continue
-                col = jnp.where(sub > s, col, 0.0)
-            left[h] = left[h] - col * row
-            right[h] = right[h] - col * row_e
+    for g in range(groups):
+        base = SUB * g
+        cols = [jnp.broadcast_to(left[g][:, base + t:base + t + 1], wide) for t in range(SUB)]
+        pivots, invs, rows, rows_e = [], [], [], []
+        for s in range(SUB):
+            scal = [jnp.broadcast_to(cols[t][s:s + 1, :], wide) for t in range(s, SUB)]
+            inv = 1.0 / scal[0]
+            mult = jnp.where(sub > s, cols[s] * inv, 0.0)
+            for t in range(s + 1, SUB):
+                cols[t] = cols[t] - mult * scal[t - s]
+            row = jnp.broadcast_to(left[g][s:s + 1, :], wide)
+            row_e = jnp.broadcast_to(right[g][s:s + 1, :], wide)
+            left[g] = left[g] - mult * row
+            right[g] = right[g] - mult * row_e
+            pivots.append(scal)
+            invs.append(inv)
+            rows.append(row)
+            rows_e.append(row_e)
+        for h in range(g + 1, groups):
+            cols = [jnp.broadcast_to(left[h][:, base + t:base + t + 1], wide) for t in range(SUB)]
+            for s in range(SUB):
+                mult = cols[s] * invs[s]
+                for t in range(s + 1, SUB):
+                    cols[t] = cols[t] - mult * pivots[s][t - s]
+                left[h] = left[h] - mult * rows[s]
+                right[h] = right[h] - mult * rows_e[s]
     for g in range(groups):
         pivot = jnp.sum(jnp.where(lane == sub + SUB * g, left[g], 0.0), axis=1, keepdims=True)
         root = jnp.sqrt(pivot)
@@ -62,7 +76,74 @@
     return jnp.concatenate(left, axis=0), jnp.concatenate(right, axis=0)
 
 
-def factor_kernel(packed_ref, atb_ref, squares_ref, tri_ref, direction_ref, alpha_ref, work, inverse):
+def split2(x):
+    hi = x.astype(jnp.bfloat16)
+    return hi, (x - hi.astype(jnp.float32)).astype(jnp.bfloat16)
+
+
+def dot_pairs(a, b, dims):
+    def one(x, y):
+        return lax.dot_general(x, y, (dims, ((), ())), preferred_element_type=jnp.float32)
+    return one(a[0], b[0]) + (one(a[0], b[1]) + one(a[1], b[0]))
+
+
+NN = ((1,), (0,))
+TT = ((0,), (0,))
+
+
+def eliminate(tiles, work, inverse, high, low, ready=None):
+    n = tiles * TILE
+
+    def step(k, carry):
+        here = pl.ds(pl.multiple_of(k * TILE, TILE), TILE)
+        for kk in range(tiles):
+            if ready is None and kk == 0:
+                continue
+
+            @pl.when(k == kk)
+            def _(kk=kk):
+                if ready is not None:
+                    ready(kk)
+                if kk:
+                    at = kk * TILE
+                    own = (high[:at, at:at + TILE], low[:at, at:at + TILE])
+                    rest = (high[:at, at:], low[:at, at:])
+                    work[at:at + TILE, at:] = work[at:at + TILE, at:] - dot_pairs(own, rest, TT)
+
+        upper, inv = factor_tile(work[here, here])
+        inverse[here, :] = inv
+        work[here, here] = upper
+        for kk in range(tiles):
+            @pl.when(k == kk)
+            def _(kk=kk):
+                at = kk * TILE
+                panel = dot_pairs(split2(inverse[at:at + TILE, :]), split2(work[at:at + TILE, at + TILE:]), NN)
+                work[at:at + TILE, at + TILE:] = panel
+                panel_high, panel_low = split2(panel)
+                high[at:at + TILE, at + TILE:] = panel_high
+                low[at:at + TILE, at + TILE:] = panel_low
+        return carry
+
+    lax.fori_loop(0, tiles, step, 0)
+
+
+def back_solve(tiles, work, inverse, high, low, direction_ref, dir_high, dir_low):
+    n = tiles * TILE
+    for k in range(tiles - 1, -1, -1):
+        at = k * TILE
+        rest = work[at:at + TILE, n:]
+        if k < tiles - 1:
+            row = (high[at:at + TILE, at + TILE:n], low[at:at + TILE, at + TILE:n])
+            rest = rest - dot_pairs(row, (dir_high[at + TILE:, :], dir_low[at + TILE:, :]), NN)
+        part = dot_pairs(split2(inverse[at:at + TILE, :]), split2(rest), TT)
+        direction_ref[at:at + TILE, :] = part
+        part_high, part_low = split2(part)
+        dir_high[at:at + TILE, :] = part_high
+        dir_low[at:at + TILE, :] = part_low
+
+
+def factor_kernel(packed_ref, atb_ref, squares_ref, tri_ref, direction_ref, alpha_ref,
+                  work, inverse, high, low, dir_high, dir_low):
     n = tri_ref.shape[0]
     tiles = n // TILE
     offset = 0
@@ -73,42 +154,14 @@
         if i:
             work[i * TILE:(i + 1) * TILE, :i * TILE] = jnp.zeros((TILE, i * TILE), jnp.float32)
     work[:, n:] = atb_ref[...]
-    width = work.shape[1]
-
-    def step(k, carry):
-        at = pl.multiple_of(k * TILE, TILE)
-        here = pl.ds(at, TILE)
-        upper, inv = factor_tile(work[here, here])
-        inverse[here, :] = inv
-        column = lax.broadcasted_iota(jnp.int32, (TILE, width), 1)
-        panel = dot_nn(inv, work[here, :])
-        work[here, :] = jnp.where(column >= at + TILE, panel, 0.0)
-        work[here, here] = upper
-
-        def trail(i, carry):
-            there = pl.ds(pl.multiple_of(i * TILE, TILE), TILE)
-            work[there, :] = work[there, :] - dot_tt(work[here, there], work[here, :])
-            return carry
-
-        return lax.fori_loop(k + 1, tiles, trail, carry)
-
-    lax.fori_loop(0, tiles, step, 0)
+    eliminate(tiles, work, inverse, high, low)
     tri_ref[...] = work[:, :n]
     beta = jnp.sqrt(squares_ref[0:1, :])
     lifted = work[:, n:] / beta
     alpha = jnp.sqrt(jnp.sum(lifted * lifted, axis=0, keepdims=True))
     alpha_ref[...] = jnp.broadcast_to(alpha, alpha_ref.shape)
     work[:, n:] = lifted / alpha
-    direction_ref[...] = jnp.zeros_like(direction_ref)
-
-    def back(t, carry):
-        k = tiles - 1 - t
-        here = pl.ds(pl.multiple_of(k * TILE, TILE), TILE)
-        rest = work[here, n:] - dot_nn(tri_ref[here, :], direction_ref[...])
-        direction_ref[here, :] = dot_tt(inverse[here, :], rest)
-        return carry
-
-    lax.fori_loop(0, tiles, back, 0)
+    back_solve(tiles, work, inverse, high, low, direction_ref, dir_high, dir_low)
 
 
 def factor_and_solve(packed, atb, squares):
@@ -125,6 +178,10 @@
         scratch_shapes=[
             pltpu.VMEM((n, n + k), jnp.float32),
             pltpu.VMEM((n, TILE), jnp.float32),
+            pltpu.VMEM((n, n + k), jnp.bfloat16),
+            pltpu.VMEM((n, n + k), jnp.bfloat16),
+            pltpu.VMEM((n, k), jnp.bfloat16),
+            pltpu.VMEM((n, k), jnp.bfloat16),
         ],
         compiler_params=pltpu.CompilerParams(vmem_limit_bytes=48 * 1024 * 1024),
         name="factor_and_solve",

time: 397 us -> 322 us (0.81)
  Pallas kernels: 119 us -> 43.2 us
    pallas_call x1, Pallas kernels: 119 us -> 43.2 us  [factor_and_solve(): pl.pallas_call(factor_kernel, out_shape=(jax.ShapeDtypeStruct((n, n), jnp...]
  transfers between devices with their start and end apart: 3 -> 3, of which waited for: 2 -> 2; matrix products, arithmetic and copies ran while one was open for 3% -> 4% of each run, Pallas kernels for 0% -> 0%
where the time goes in v1:
time: 322 us; the launch traced here: 321 us
  waiting for transfers between devices  181 us (56%)
  Pallas kernels  43.2 us (13%)
  matrix products  28.3 us (9%)
  local copies, waits for them, and re-layouts  26.7 us (8%)
  between operations  14.2 us (4%)
  starting transfers between devices  13.5 us (4%)
  blocking collectives  10.4 us (3%)
  other arithmetic  3.48 us (1%)
    psum x1, waiting for transfers between devices, shards(): packed = lax.psum(jnp.concatenate(tiles, axis=0), AXES)  137 us
    all_to_all x1, waiting for transfers between devices, shards(): turned = lax.all_to_all(mixed, AXES, 0, 0, tiled=True)  44.1 us
    pallas_call x1, Pallas kernels, factor_and_solve(): pl.pallas_call(factor_kernel, out_shape=(jax.ShapeDtypeStruct((n, n), jnp...  43.2 us
    unnamed x46, local copies, waits for them, and re-layouts  25.9 us
    dot_general x3, matrix products, dot_nn(): lax.dot_general(a, b, (((1,), (0,)), ((), ())), precision=exact_mode, pre...  15.9 us
    dot_general x9, matrix products, dot_tt(): lax.dot_general(a, b, (((0,), (0,)), ((), ())), precision=exact_mode, pre...  12.4 us
    all_to_all x1, blocking collectives, shards(): lax.all_to_all(jnp.broadcast_to(gamma_part, (devices, rhs.shape[1])), AXE...  10.4 us
    all_to_all x1, starting transfers between devices, shards(): small = lax.all_to_all(small, AXES, 0, 0, tiled=True)  7.33 us
  transfers between devices with their start and end apart: 3, of which 2 were waited for; matrix products, arithmetic and copies ran while one was open for 4% of the time, Pallas kernels for 0%

profile of v1, /device:TPU:0, one launch (start us, length us, event | category | flops | bytes accessed | tf_op | source)
XLA Modules:
  0.0 321.1 jit_solution(1601952491248520813)
XLA Ops:
  7.2 0.7 and_select_fusion
  8.0 1.0 multiply_reduce_fusion.1
  9.1 0.6 all_to_all.23
  9.7 7.3 %all-to-all-start.1 = ((f32[32,1,144]{2,1,0:T(1,128)}), f32[32,1,144]{2,1,0:T(1,128)S(1)}, u32[]{:S(2)}, u32[]{:S(2)}) async-start(f32[32,1,144]{2,1,0:T(1,128)} %all_to_all.23), calls=%async_computation.1 | async-start | bytes 65536 | tf_op jit(solution)/shard_map/all_to_all | solution.py:212
  17.0 0.7 convert_element_type.6
  17.7 7.8 %fusion = f32[512,1024]{1,0:T(8,128)} fusion(f32[512,1024]{1,0:T(8,128)} %param.4, f32[512]{0:T(512)S(1)} %convert_element_type.6), kind=kOutput, calls=%fused_computation.5 | convolution fusion | flops 3232235520 | bytes 4196352 | tf_op jit(solution)/shard_map/dot_general | solution.py:34
  25.5 6.0 %all-to-all-start = ((f32[32,16,1024]{2,1,0:T(8,128)}), f32[32,16,1024]{2,1,0:T(8,128)}, u32[]{:S(2)}, u32[]{:S(2)}) async-start(f32[32,16,1024]{2,1,0:T(8,128)} %bitcast.34), calls=%async_computation | async-start | bytes 4194304 | tf_op jit(solution)/shard_map/all_to_all | solution.py:221
  31.8 4.2 %fusion.102 = f32[1024,128]{1,0:T(8,128)} fusion(f32[512,1024]{1,0:T(8,128)S(1)} %copy-done.2, f32[512,128]{1,0:T(8,128)S(1)} %copy-done.3), kind=kOutput, calls=%fused_computation.170 | convolution fusion | flops 805306368 | bytes 2883584 | tf_op jit(solution)/shard_map/dot_general | solution.py:29
  36.1 44.1 %all-to-all-done = f32[32,16,1024]{2,1,0:T(8,128)} async-done(((f32[32,16,1024]{2,1,0:T(8,128)}), f32[32,16,1024]{2,1,0:T(8,128)}, u32[]{:S(2)}, u32[]{:S(2)}) %all-to-all-start) | async-done | bytes 2097184 | tf_op jit(solution)/shard_map/all_to_all | solution.py:221
  80.2 6.1 %broadcast_multiply_fusion = (f32[512,1024]{1,0:T(8,128)S(1)}, f32[512,1024]{1,0:T(8,128)S(1)}) fusion(f32[512]{0:T(512)S(1)} %mul.76, f32[512,1024]{1,0:T(8,128)} %bitcast.1, s32[512]{0:T(512)S(1)} %get-tuple-element.30, s32[512]{0:T(512)S(1)} %get-tuple-element.31), kind=kOutput, calls=%fused_computation.36 | convolution fusion | flops 3229614080 | bytes 6297600 | tf_op jit(solution)/shard_map/dot_general | solution.py:34
  86.4 1.3 fusion.72
  87.7 1.2 fusion.2
  88.9 1.1 fusion.4
  90.0 1.0 fusion.6
  91.0 1.0 fusion.21
  92.0 0.7 fusion.37
  93.4 0.6 constant_dynamic-update-slice_fusion.34
  94.0 0.6 constant_dynamic-update-slice_fusion.33
  95.3 0.6 constant_dynamic-update-slice_fusion.31
  95.9 0.6 constant_dynamic-update-slice_fusion.30
  96.6 0.6 constant_dynamic-update-slice_fusion.29
  97.2 0.6 constant_dynamic-update-slice_fusion.28
  97.9 0.6 constant_dynamic-update-slice_fusion.27
  115.6 1.2 convolution_dynamic-update-slice_fusion
  117.1 137.1 %all-reduce.3.cloned.1.call-done = (f32[4608,128]{1,0:T(8,128)}, f32[1024,128]{1,0:T(8,128)}) async-done(((f32[4608,128]{1,0:T(8,128)}, f32[1024,128]{1,0:T(8,128)}), (f32[4608,128]{1,0:T(8,128)}, f32[1024,128]{1,0:T(8,128)})) %all-reduce.3.cloned.1.call-update) | async-done | bytes 2883600 | tf_op jit(solution)/shard_map/psum | solution.py:233
  254.2 1.7 copy-done
  255.8 1.0 copy-done.1
  256.9 43.2 %factor_and_solve.1 = (f32[1024,1024]{1,0:T(8,128)}, f32[1024,128]{1,0:T(8,128)S(1)}, f32[8,128]{1,0:T(8,128)S(1)}) custom-call(f32[4608,128]{1,0:T(8,128)S(1)} %copy-done, f32[1024,128]{1,0:T(8,128)S(1)} %copy-done.1, f32[8,128]{1,0:T(8,128)S(1)} %broadcast_in_dim.25.squares_ref), custom_call_target="tpu_custom_call" | custom-call | tf_op jit(solution)/shard_map/factor_and_solve/pallas_call | solution.py:169
  300.1 2.0 multiply_reduce_fusion
  302.1 10.4 %all_to_all.30 = f32[32,1,128]{2,1,0:T(1,128)S(1)} all-to-all(f32[32,1,128]{2,1,0:T(1,128)S(1)} %broadcast_in_dim.26), channel_id=1, replica_groups=mesh['rows'=8,'grp'=4] {'rows','grp'}, dimensions={0} | all-to-all | bytes 32768 | tf_op jit(solution)/shard_map/all_to_all | solution.py:241
  312.5 0.8 broadcast_multiply_fusion.1
  313.5 0.8 copy.22
  (55 shorter events, 19.2 us)
Async XLA Ops:
  9.7 15.8 %all-to-all-start.1 = ((f32[32,1,144]{2,1,0:T(1,128)}), f32[32,1,144]{2,1,0:T(1,128)S(1)}, u32[]{:S(2)}, u32[]{:S(2)}) async-start(f32[32,1,144]{2,1,0:T(1,128)} %all_to_all.23), calls=%async_computation.1 | async-start | bytes 65536 | tf_op jit(solution)/shard_map/all_to_all | solution.py:212
  25.5 6.2 %copy-start.2 = (f32[512,1024]{1,0:T(8,128)S(1)}, f32[512,1024]{1,0:T(8,128)}, u32[]{:S(2)}) copy-start(f32[512,1024]{1,0:T(8,128)} %param.4) | copy-start | bytes 6291460
  25.5 6.2 %copy-start.3 = (f32[512,128]{1,0:T(8,128)S(1)}, f32[512,128]{1,0:T(8,128)}, u32[]{:S(2)}) copy-start(f32[512,128]{1,0:T(8,128)} %param.7) | copy-start | bytes 786436
  25.5 54.7 %all-to-all-start = ((f32[32,16,1024]{2,1,0:T(8,128)}), f32[32,16,1024]{2,1,0:T(8,128)}, u32[]{:S(2)}, u32[]{:S(2)}) async-start(f32[32,16,1024]{2,1,0:T(8,128)} %bitcast.34), calls=%async_computation | async-start | bytes 4194304 | tf_op jit(solution)/shard_map/all_to_all | solution.py:221
  31.5 222.7 %all-reduce.3.cloned.1.call-start = ((), (), s32[]{:S(2)}) async-start(), calls=%async_computation.3 | async-start | bytes 5767168 | tf_op jit(solution)/shard_map/psum | solution.py:233
  254.2 1.7 copy-start
  255.8 1.0 copy-start.1
Sparse Core Ops, SparseCore 0:
  117.0 137.1 all-reduce.2

commit v2 on v1

v2 whole, which is shorter than its diff:
```python
import functools
import math

import jax
import jax.numpy as jnp
from jax import lax
from jax.experimental import pallas as pl
from jax.experimental.pallas import tpu as pltpu
from jax.sharding import PartitionSpec as P

TILE = 128
SUB = 8
AXES = ("rows", "grp")
MESH = pl.DeviceIdType.MESH


def place():
    grp = lax.axis_size("grp")
    return lax.axis_index("rows") * grp + lax.axis_index("grp")


def coords(index):
    grp = lax.axis_size("grp")
    return (index // grp, lax.rem(index, grp))


def send(src, dst, send_sem, recv_sem, target):
    pltpu.make_async_remote_copy(src_ref=src, dst_ref=dst, send_sem=send_sem, recv_sem=recv_sem,
                                 device_id=coords(target), device_id_type=MESH).start()


def await_bytes(ref, sem):
    pltpu.make_async_copy(ref, ref, sem).wait()


def greet(devices, me):
    barrier = pltpu.get_barrier_semaphore()

    def one(d, carry):
        pl.semaphore_signal(barrier, inc=1, device_id=coords(lax.rem(me + d, devices)), device_id_type=MESH)
        return carry

    lax.fori_loop(1, devices, one, 0)
    return barrier


def loop(start, stop, body):
    def one(i, carry):
        body(i)
        return carry

    lax.fori_loop(start, stop, one, 0)


def factor_tile(block):
    groups = TILE // SUB
    lane = lax.broadcasted_iota(jnp.int32, (SUB, TILE), 1)
    sub = lax.broadcasted_iota(jnp.int32, (SUB, TILE), 0)
    wide = (SUB, TILE)
    left = [block[SUB * g:SUB * (g + 1), :] for g in range(groups)]
    right = [(lane == sub + SUB * g).astype(jnp.float32) for g in range(groups)]
    for g in range(groups):
        base = SUB * g
        cols = [jnp.broadcast_to(left[g][:, base + t:base + t + 1], wide) for t in range(SUB)]
        pivots, invs, rows, rows_e = [], [], [], []
        for s in range(SUB):
            scal = [jnp.broadcast_to(cols[t][s:s + 1, :], wide) for t in range(s, SUB)]
            inv = 1.0 / scal[0]
            mult = jnp.where(sub > s, cols[s] * inv, 0.0)
            for t in range(s + 1, SUB):
                cols[t] = cols[t] - mult * scal[t - s]
            row = jnp.broadcast_to(left[g][s:s + 1, :], wide)
            row_e = jnp.broadcast_to(right[g][s:s + 1, :], wide)
            left[g] = left[g] - mult * row
            right[g] = right[g] - mult * row_e
            pivots.append(scal)
            invs.append(inv)
            rows.append(row)
            rows_e.append(row_e)
        for h in range(g + 1, groups):
            cols = [jnp.broadcast_to(left[h][:, base + t:base + t + 1], wide) for t in range(SUB)]
            for s in range(SUB):
                mult = cols[s] * invs[s]
                for t in range(s + 1, SUB):
                    cols[t] = cols[t] - mult * pivots[s][t - s]
                left[h] = left[h] - mult * rows[s]
                right[h] = right[h] - mult * rows_e[s]
    for g in range(groups):
        pivot = jnp.sum(jnp.where(lane == sub + SUB * g, left[g], 0.0), axis=1, keepdims=True)
        root = jnp.sqrt(pivot)
        left[g] = jnp.where(lane >= sub + SUB * g, left[g] / root, 0.0)
        right[g] = jnp.where(lane <= sub + SUB * g, right[g] / root, 0.0)
    return jnp.concatenate(left, axis=0), jnp.concatenate(right, axis=0)


def dot_tt(a, b):
    return lax.dot_general(a, b, (TT, ((), ())), preferred_element_type=jnp.float32)


def split2(x):
    hi = x.astype(jnp.bfloat16)
    return hi, (x - hi.astype(jnp.float32)).astype(jnp.bfloat16)


def dot_pairs(a, b, dims):
    def one(x, y):
        return lax.dot_general(x, y, (dims, ((), ())), preferred_element_type=jnp.float32)
    return one(a[0], b[0]) + (one(a[0], b[1]) + one(a[1], b[0]))


NN = ((1,), (0,))
TT = ((0,), (0,))


def eliminate(tiles, work, inverse, high, low, ready, panel_ready):

    def step(k, carry):
        here = pl.ds(pl.multiple_of(k * TILE, TILE), TILE)
        for kk in range(tiles):
            @pl.when(k == kk)
            def _(kk=kk):
                ready(kk)
                if kk:
                    at = kk * TILE
                    own = (high[:at, at:at + TILE], low[:at, at:at + TILE])
                    rest = (high[:at, at:], low[:at, at:])
                    work[at:at + TILE, at:] = work[at:at + TILE, at:] - dot_pairs(own, rest, TT)

        upper, inv = factor_tile(work[here, here])
        inverse[here, :] = inv
        work[here, here] = upper
        for kk in range(tiles):
            @pl.when(k == kk)
            def _(kk=kk):
                at = kk * TILE
                panel_ready(kk)
                panel = dot_pairs(split2(inverse[at:at + TILE, :]), split2(work[at:at + TILE, at + TILE:]), NN)
                work[at:at + TILE, at + TILE:] = panel
                panel_high, panel_low = split2(panel)
                high[at:at + TILE, at + TILE:] = panel_high
                low[at:at + TILE, at + TILE:] = panel_low
        return carry

    lax.fori_loop(0, tiles, step, 0)


def back_solve(tiles, work, inverse, high, low, direction_ref, dir_high, dir_low):
    n = tiles * TILE
    for k in range(tiles - 1, -1, -1):
        at = k * TILE
        rest = work[at:at + TILE, n:]
        if k < tiles - 1:
            row = (high[at:at + TILE, at + TILE:n], low[at:at + TILE, at + TILE:n])
            rest = rest - dot_pairs(row, (dir_high[at + TILE:, :], dir_low[at + TILE:, :]), NN)
        part = dot_pairs(split2(inverse[at:at + TILE, :]), split2(rest), TT)
        direction_ref[at:at + TILE, :] = part
        part_high, part_low = split2(part)
        dir_high[at:at + TILE, :] = part_high
        dir_low[at:at + TILE, :] = part_low


def tile_of(t, tiles):
    row, offset = 0, 0
    start = 0
    for r in range(1, tiles):
        start = start + tiles - r + 1
        past = (t - start + tiles * tiles) // (tiles * tiles)
        row = row + past
        offset = offset + past * (tiles - r + 1)
    return row, t - offset + row


def parity(value, bits):
    width = 1
    while width < bits:
        width *= 2
    while width > 1:
        width //= 2
        value = value ^ (value >> width)
    return value & 1


def mix_kernel(mat_ref, signs_ref, picks_ref, rhs_ref, out_ref,
               signed, dense, picks_all, table, mixed_high, mixed_low, partial, landed, sketch,
               atb_send, atb_land, picks_out, send_sem, recv_sem, layer_sem):
    devices = picks_all.shape[0]
    planes, depth, _ = landed.shape
    tiles, rows, _ = dense.shape
    samp = depth // tiles
    per = TILE // samp
    me = place()
    z, q = me // tiles, lax.rem(me, tiles)
    scale = 1.0 / math.sqrt(samp * devices)

    barrier = greet(devices, me)
    sign = signs_ref[...]
    for p in range(tiles):
        signed[p] = mat_ref[:, p * TILE:(p + 1) * TILE] * sign
    picks_out[...] = picks_ref[...]
    picks_all[me] = picks_ref[...]
    pl.semaphore_wait(barrier, devices - 1)

    def send_picks(d):
        send(picks_out, picks_all.at[me], send_sem.at[0], recv_sem.at[0], lax.rem(me + d, devices))

    loop(1, devices, send_picks)

    def send_dense(d):
        p = lax.rem(q + d, tiles)
        send(signed.at[p], dense.at[q], send_sem.at[1], recv_sem.at[1], z * tiles + p)

    loop(1, tiles, send_dense)
    dense[q] = signed[q]

    rhs = rhs_ref[...]
    rhs_pair = split2(rhs)
    squares = jnp.broadcast_to(jnp.sum(rhs * rhs, axis=0, keepdims=True), (SUB, TILE))

    def atb_tile(p):
        at = pl.multiple_of(p * TILE, TILE)
        atb_send[p, :TILE, :] = dot_pairs(split2(mat_ref[:, pl.ds(at, TILE)]), rhs_pair, TT)
        atb_send[p, TILE:, :] = squares

    loop(0, tiles, atb_tile)
    atb_land[q] = atb_send[q]

    def send_atb(d):
        p = lax.rem(q + d, tiles)
        send(atb_send.at[p], atb_land.at[q], send_sem.at[2], recv_sem.at[2], z * tiles + p)

    loop(1, tiles, send_atb)

    await_bytes(picks_all.at[pl.ds(0, devices - 1)], recv_sem.at[0])
    lane = lax.broadcasted_iota(jnp.int32, (1, TILE), 1)

    def fill_table(c):
        group, qk = c // tiles, lax.rem(c, tiles)
        row = picks_all[group * per * tiles + qk]
        for e in range(1, per):
            row = jnp.where(lane >= e * samp, picks_all[(group * per + e) * tiles + qk], row)
        counter = lax.broadcasted_iota(jnp.int32, (rows, TILE), 0)
        odd = parity(counter & row, (rows - 1).bit_length())
        table[c] = (1 - 2 * odd).astype(jnp.float32).astype(jnp.bfloat16)

    loop(0, planes // per * tiles, fill_table)

    await_bytes(dense.at[pl.ds(0, tiles - 1)], recv_sem.at[1])
    chunk = 32

    def butterfly(c):
        here = pl.ds(pl.multiple_of(c * chunk, chunk), chunk)
        parts = [dense[d, here, :] for d in range(tiles)]
        span = 1
        while span < tiles:
            parts = [parts[d] + parts[d + span] if d // span % 2 == 0 else parts[d - span] - parts[d]
                     for d in range(tiles)]
            span *= 2
        for d in range(tiles):
            high, low = split2(parts[d])
            mixed_high[d, here, :] = high
            mixed_low[d, here, :] = low

    loop(0, rows // chunk, butterfly)

    def project(qk):
        here = pl.ds(pl.multiple_of(qk * samp, samp), samp)
        for group in range(planes // per):
            rows_of = table[group * tiles + qk]
            block = dot_tt(rows_of, mixed_high[qk]) + dot_tt(rows_of, mixed_low[qk])
            for e in range(per):
                zk = group * per + e
                odd = 0
                for bit in range(planes.bit_length() - 1):
                    if zk >> bit & 1:
                        odd = odd + lax.rem(z // (1 << bit), 2)
                flip = 1.0 - 2.0 * jnp.asarray(lax.rem(jnp.asarray(odd, jnp.int32), 2), jnp.float32)
                partial[zk, here, :] = block[e * samp:(e + 1) * samp, :] * (flip * scale)
        landed[z, here, :] = partial[z, here, :]

        def send_layer(d):
            zk = lax.rem(z + d, planes)
            send(partial.at[zk, here], landed.at[z, here], send_sem.at[3], layer_sem.at[qk], zk * tiles + q)

        loop(1, planes, send_layer)

    loop(0, tiles, project)

    def combine(qk):
        here = pl.ds(pl.multiple_of(qk * samp, samp), samp)
        await_bytes(landed.at[pl.ds(0, planes - 1), here], layer_sem.at[qk])
        sketch[q, here, :] = jnp.sum(landed[:, here, :], axis=0)

        def send_sketch(d):
            p = lax.rem(q + d, tiles)
            send(sketch.at[q, here], sketch.at[q, here], send_sem.at[4], recv_sem.at[4], z * tiles + p)

        loop(1, tiles, send_sketch)

    loop(0, tiles, combine)

    await_bytes(atb_land.at[pl.ds(0, tiles - 1)], recv_sem.at[2])
    slots = out_ref.shape[0] - 1
    out_ref[slots] = jnp.sum(atb_land[...], axis=0)

    await_bytes(sketch.at[pl.ds(0, tiles - 1)], recv_sem.at[4])

    def gram_tile(s):
        t = jnp.minimum(s * tiles + q, tiles * (tiles + 1) // 2 - 1)
        i, j = tile_of(t, tiles)
        out_ref[s, :TILE, :] = dot_pairs(split2(sketch[i]), split2(sketch[j]), TT)
        out_ref[s, TILE:, :] = jnp.zeros((SUB, TILE), jnp.float32)

    loop(0, slots, gram_tile)

    def drain(d):
        await_bytes(picks_out, send_sem.at[0])

    loop(1, devices, drain)
    await_bytes(dense.at[pl.ds(0, tiles - 1)], send_sem.at[1])
    await_bytes(atb_land.at[pl.ds(0, tiles - 1)], send_sem.at[2])
    await_bytes(partial.at[pl.ds(0, planes - 1)], send_sem.at[3])
    await_bytes(sketch.at[pl.ds(0, tiles - 1)], send_sem.at[4])


def mix(mat, signs, picks, rhs, devices):
    rows, n = mat.shape
    tiles = n // TILE
    samp = picks.shape[0]
    planes = devices // tiles
    per = TILE // samp
    slots = (tiles * (tiles + 1) // 2 + tiles - 1) // tiles
    vmem = pl.BlockSpec(memory_space=pltpu.VMEM)
    f32, bf16 = jnp.float32, jnp.bfloat16
    sign_column = signs.astype(f32).reshape(rows, 1)
    picks_row = jnp.tile(picks % rows, per).reshape(1, TILE)
    return pl.pallas_call(
        mix_kernel,
        out_shape=jax.ShapeDtypeStruct((slots + 1, TILE + SUB, TILE), f32),
        in_specs=[vmem] * 4,
        out_specs=vmem,
        scratch_shapes=[
            pltpu.VMEM((tiles, rows, TILE), f32),
            pltpu.VMEM((tiles, rows, TILE), f32),
            pltpu.VMEM((devices, 1, TILE), jnp.int32),
            pltpu.VMEM((planes // per * tiles, rows, TILE), bf16),
            pltpu.VMEM((tiles, rows, TILE), bf16),
            pltpu.VMEM((tiles, rows, TILE), bf16),
            pltpu.VMEM((planes, tiles * samp, TILE), f32),
            pltpu.VMEM((planes, tiles * samp, TILE), f32),
            pltpu.VMEM((tiles, tiles * samp, TILE), f32),
            pltpu.VMEM((tiles, TILE + SUB, TILE), f32),
            pltpu.VMEM((tiles, TILE + SUB, TILE), f32),
            pltpu.VMEM((1, TILE), jnp.int32),
            pltpu.SemaphoreType.DMA((5,)),
            pltpu.SemaphoreType.DMA((5,)),
            pltpu.SemaphoreType.DMA((tiles,)),
        ],
        compiler_params=pltpu.CompilerParams(
            collective_id=0, has_side_effects=True, vmem_limit_bytes=56 * 1024 * 1024),
        name="mix",
    )(mat, sign_column, picks_row, rhs)


def solve_kernel(part_ref, mat_ref, rhs_ref, tri_ref, solution_ref, residual_ref,
                 landed, gathered, work, inverse, high, low, mat_high, mat_low, direction, dir_high, dir_low,
                 squares, gamma_out, gamma_all, send_sem, layer_sem, plane_sem, gamma_sem, tri_sem):
    planes = landed.shape[0]
    tiles, slots = gathered.shape[0], gathered.shape[1] - 1
    n = tiles * TILE
    devices = planes * tiles
    me = place()
    z, q = me // tiles, lax.rem(me, tiles)
    height = [TILE] * slots + [TILE + SUB]
    order = [0, slots] + list(range(1, slots))

    barrier = greet(devices, me)
    for i in range(1, tiles):
        work[i * TILE:(i + 1) * TILE, :i * TILE] = jnp.zeros((TILE, i * TILE), jnp.float32)
    for s in range(slots + 1):
        landed[z, s] = part_ref[s]
    pl.semaphore_wait(barrier, devices - 1)
    for s in order:
        def send_layer(d, s=s):
            zk = lax.rem(z + d, planes)
            send(part_ref.at[s, :height[s]], landed.at[z, s, :height[s]], send_sem.at[0], layer_sem.at[s],
                 zk * tiles + q)

        loop(1, planes, send_layer)

    mat_high[...], mat_low[...] = split2(mat_ref[...])

    def advance(s):
        await_bytes(landed.at[pl.ds(0, planes - 1), s, :height[s]], layer_sem.at[s])
        total = jnp.sum(landed[:, s, :height[s], :], axis=0)
        gathered[q, s] = total[:TILE]
        if s == slots:
            squares[...] = total[TILE:]

        def send_plane(d):
            p = lax.rem(q + d, tiles)
            send(gathered.at[q, s], gathered.at[q, s], send_sem.at[1], plane_sem.at[s], z * tiles + p)

        loop(1, tiles, send_plane)

    def take(s):
        await_bytes(gathered.at[pl.ds(0, tiles - 1), s], plane_sem.at[s])
        for p in range(tiles):
            if s == slots:
                work[p * TILE:(p + 1) * TILE, n:] = gathered[p, s]
            elif s * tiles + p < tiles * (tiles + 1) // 2:
                i, j = tile_of(s * tiles + p, tiles)
                work[i * TILE:(i + 1) * TILE, j * TILE:(j + 1) * TILE] = gathered[p, s]

    last = [tile_of_end(k, tiles) // tiles for k in range(tiles)]
    moves, panel_moves = [[] for _ in range(tiles)], [[] for _ in range(tiles)]
    moves[0] = [(advance, 0), (advance, slots), (take, 0)]
    panel_moves[0] = [(advance, 1), (take, slots)]
    taken, sent = 0, 1
    for k in range(1, tiles):
        want = last[min(k + 1, tiles - 1)]
        while sent < want:
            sent += 1
            moves[k].append((advance, sent))
        while taken < last[k]:
            taken += 1
            moves[k].append((take, taken))

    def run(todo):
        for action, s in todo:
            action(s)

    def ready(k):
        if k:
            done = slice((k - 1) * TILE, k * TILE)
            pltpu.make_async_copy(work.at[done, :n], tri_ref.at[done], tri_sem).start()
        run(moves[k])

    eliminate(tiles, work, inverse, high, low, ready, lambda k: run(panel_moves[k]))
    final = slice(n - TILE, n)
    pltpu.make_async_copy(work.at[final, :n], tri_ref.at[final], tri_sem).start()

    beta = jnp.sqrt(squares[0:1, :])
    lifted = work[:, n:] / beta
    alpha = jnp.sqrt(jnp.sum(lifted * lifted, axis=0, keepdims=True))
    work[:, n:] = lifted / alpha
    back_solve(tiles, work, inverse, high, low, direction, dir_high, dir_low)

    rhs = rhs_ref[...]
    image = dot_pairs((mat_high[...], mat_low[...]), (dir_high[...], dir_low[...]), NN)
    pushed = image - alpha / beta * rhs
    gamma_out[...] = jnp.sum(pushed * pushed, axis=0, keepdims=True)
    gamma_all[me] = gamma_out[...]

    def send_gamma(d):
        send(gamma_out, gamma_all.at[me], send_sem.at[2], gamma_sem, lax.rem(me + d, devices))

    loop(1, devices, send_gamma)
    await_bytes(gamma_all.at[pl.ds(0, devices - 1)], gamma_sem)
    gamma = jnp.sqrt(jnp.sum(gamma_all[...], axis=0))
    coef = beta * alpha / (alpha * alpha + gamma * gamma)
    solution_ref[...] = direction[...] * coef
    residual_ref[...] = rhs - image * coef

    for s in range(slots + 1):
        await_bytes(landed.at[pl.ds(0, planes - 1), s, :height[s]], send_sem.at[0])
        await_bytes(gathered.at[pl.ds(0, tiles - 1), s], send_sem.at[1])
    await_bytes(gamma_all.at[pl.ds(0, devices - 1)], send_sem.at[2])
    pltpu.make_async_copy(work.at[:, :n], tri_ref, tri_sem).wait()


def tile_of_end(row, tiles):
    return sum(tiles - r for r in range(row + 1)) - 1


def solve(part, mat, rhs, devices):
    rows, n = mat.shape
    tiles = n // TILE
    planes = devices // tiles
    slots = part.shape[0] - 1
    vmem = pl.BlockSpec(memory_space=pltpu.VMEM)
    f32, bf16 = jnp.float32, jnp.bfloat16
    return pl.pallas_call(
        solve_kernel,
        out_shape=(
            jax.ShapeDtypeStruct((n, n), f32),
            jax.ShapeDtypeStruct((n, TILE), f32),
            jax.ShapeDtypeStruct((rows, TILE), f32),
        ),
        in_specs=[vmem] * 3,
        out_specs=(pl.BlockSpec(memory_space=pl.ANY), vmem, vmem),
        scratch_shapes=[
            pltpu.VMEM((planes, slots + 1, TILE + SUB, TILE), f32),
            pltpu.VMEM((tiles, slots + 1, TILE, TILE), f32),
            pltpu.VMEM((n, n + TILE), f32),
            pltpu.VMEM((n, TILE), f32),
            pltpu.VMEM((n, n + TILE), bf16),
            pltpu.VMEM((n, n + TILE), bf16),
            pltpu.VMEM((rows, n), bf16),
            pltpu.VMEM((rows, n), bf16),
            pltpu.VMEM((n, TILE), f32),
            pltpu.VMEM((n, TILE), bf16),
            pltpu.VMEM((n, TILE), bf16),
            pltpu.VMEM((SUB, TILE), f32),
            pltpu.VMEM((1, TILE), f32),
            pltpu.VMEM((devices, 1, TILE), f32),
            pltpu.SemaphoreType.DMA((3,)),
            pltpu.SemaphoreType.DMA((slots + 1,)),
            pltpu.SemaphoreType.DMA((slots + 1,)),
            pltpu.SemaphoreType.DMA,
            pltpu.SemaphoreType.DMA,
        ],
        compiler_params=pltpu.CompilerParams(
            collective_id=1, has_side_effects=True, vmem_limit_bytes=56 * 1024 * 1024),
        name="factor_and_solve",
    )(part, mat, rhs)


def shards(mat, signs, picks, rhs):
    devices = lax.axis_size("rows") * lax.axis_size("grp")
    part = mix(mat, signs, picks, rhs, devices)
    return solve(part, mat, rhs, devices)


def solution(mesh):
    return jax.shard_map(
        shards,
        mesh=mesh,
        in_specs=(P(AXES, None), P(AXES), P(AXES), P(AXES, None)),
        out_specs=(P(), P(), P(AXES, None)),
        check_vma=False,
    )
```

time: 322 us -> 163 us (0.51)
  waiting for transfers between devices: 181 us -> 0 us
  Pallas kernels: 43.2 us -> 153 us
  matrix products: 28.3 us -> 0 us
  local copies, waits for them, and re-layouts: 26.7 us -> 7.82 us
  between operations: 14.2 us -> 0.67 us
  starting transfers between devices: 13.5 us -> 0 us
  blocking collectives: 10.4 us -> 0 us
    psum x1 -> x0, waiting for transfers between devices: 137 us -> none  [shards(): packed = lax.psum(jnp.concatenate(tiles, axis=0), AXES)]
    pallas_call x1 -> x2, Pallas kernels: 43.2 us -> 153 us  [the longest x1 87.3 us: solve(): pl.pallas_call(solve_kernel, out_shape=(jax.ShapeDtypeStruct((n, n), f32)...]
    all_to_all x2 -> x0, waiting for transfers between devices: 44.1 us -> none  [the longest x1 44.1 us: shards(): turned = lax.all_to_all(mixed, AXES, 0, 0, tiled=True)]
    dot_general x12 -> x0, matrix products: 28.3 us -> none  [the longest x3 15.9 us: dot_nn(): lax.dot_general(a, b, (((1,), (0,)), ((), ())), precision=exact_mode, pre...]
    unnamed x46 -> x7, local copies, waits for them, and re-layouts: 25.9 us -> 6.36 us
    all_to_all x2 -> x0, starting transfers between devices: 13.3 us -> none  [the longest x1 7.33 us: shards(): small = lax.all_to_all(small, AXES, 0, 0, tiled=True)]
    all_to_all x1 -> x0, blocking collectives: 10.4 us -> none  [shards(): lax.all_to_all(jnp.broadcast_to(gamma_part, (devices, rhs.shape[1])), AXE...]
  transfers between devices with their start and end apart: 3 -> 0, of which waited for: 2 -> 0; matrix products, arithmetic and copies ran while one was open for 4% -> 0% of each run, Pallas kernels for 0% -> 0%
where the time goes in v2:
time: 163 us; the launch traced here: 162 us
  Pallas kernels  153 us (94%)
  local copies, waits for them, and re-layouts  7.82 us (5%)
    pallas_call x1, Pallas kernels, solve(): pl.pallas_call(solve_kernel, out_shape=(jax.ShapeDtypeStruct((n, n), f32)...  87.3 us
    pallas_call x1, Pallas kernels, mix(): pl.pallas_call(mix_kernel, out_shape=jax.ShapeDtypeStruct((slots + 1, TIL...  65.2 us
    unnamed x7, local copies, waits for them, and re-layouts  6.36 us

profile of v2, /device:TPU:0, one launch (start us, length us, event | category | flops | bytes accessed | tf_op | source)
XLA Modules:
  0.0 162.4 jit_solution(4282094265557044271)
XLA Ops:
  0.6 0.7 and_select_fusion
  1.3 0.6 reshape_tile.3.picks_ref
  1.9 0.7 convert_element_type.3
  2.6 0.9 copy.7.signs_ref
  3.4 65.2 %mix.1.part_ref = f32[6,136,128]{2,1,0:T(8,128)} custom-call(f32[512,1024]{1,0:T(8,128)} %mat_ref.3, f32[512,1]{1,0:T(8,128)} %copy.7.signs_ref, s32[1,128]{1,0:T(1,128)} %reshape_tile.3.picks_ref, f32[512,128]{1,0:T(8,128)} %rhs_ref.3), custom_call_target="tpu_custom_call" | custom-call | tf_op jit(solution)/shard_map/mix/pallas_call | solution.py:336
  68.6 87.3 %factor_and_solve.1 = (f32[1024,1024]{1,0:T(8,128)}, f32[1024,128]{1,0:T(8,128)}, f32[512,128]{1,0:T(8,128)}) custom-call(f32[6,136,128]{2,1,0:T(8,128)} %mix.1.part_ref, f32[512,1024]{1,0:T(8,128)} %mat_ref.3, f32[512,128]{1,0:T(8,128)} %rhs_ref.3), custom_call_target="tpu_custom_call" | custom-call | tf_op jit(solution)/shard_map/factor_and_solve/pallas_call | solution.py:482
  156.0 0.0 copy-start
  156.0 0.0 copy-start.1
  156.0 4.9 %copy.11 = f32[1024,1024]{1,0:T(8,128)} copy(f32[1024,1024]{1,0:T(8,128)} %get-tuple-element.6) | data formatting | bytes 8388608
  160.9 0.0 copy-done
  160.9 0.8 copy.12
  161.7 0.0 copy-done.1
  161.7 0.7 copy.13
  (1 shorter events, 0.0 us)
Async XLA Ops:
  156.0 4.9 %copy-start = (f32[1024,128]{1,0:T(8,128)S(1)}, f32[1024,128]{1,0:T(8,128)}, u32[]{:S(2)}) copy-start(f32[1024,128]{1,0:T(8,128)} %get-tuple-element.7) | copy-start | bytes 1572868
  156.0 5.7 %copy-start.1 = (f32[512,128]{1,0:T(8,128)S(1)}, f32[512,128]{1,0:T(8,128)}, u32[]{:S(2)}) copy-start(f32[512,128]{1,0:T(8,128)} %get-tuple-element.8) | copy-start | bytes 786436

commit v3 on v2

v3 whole, which is shorter than its diff:
```python
import functools
import math

import jax
import jax.numpy as jnp
from jax import lax
from jax.experimental import pallas as pl
from jax.experimental.pallas import tpu as pltpu
from jax.sharding import PartitionSpec as P

TILE = 128
SUB = 8
AXES = ("rows", "grp")
MESH = pl.DeviceIdType.MESH


def place():
    grp = lax.axis_size("grp")
    return lax.axis_index("rows") * grp + lax.axis_index("grp")


def coords(index):
    grp = lax.axis_size("grp")
    return (index // grp, lax.rem(index, grp))


def send(src, dst, send_sem, recv_sem, target):
    pltpu.make_async_remote_copy(src_ref=src, dst_ref=dst, send_sem=send_sem, recv_sem=recv_sem,
                                 device_id=coords(target), device_id_type=MESH).start()


def await_bytes(ref, sem):
    pltpu.make_async_copy(ref, ref, sem).wait()


def greet(devices, me):
    barrier = pltpu.get_barrier_semaphore()

    def one(d, carry):
        pl.semaphore_signal(barrier, inc=1, device_id=coords(lax.rem(me + d, devices)), device_id_type=MESH)
        return carry

    lax.fori_loop(1, devices, one, 0)
    return barrier


def loop(start, stop, body):
    def one(i, carry):
        body(i)
        return carry

    lax.fori_loop(start, stop, one, 0)


def factor_tile(block):
    groups = TILE // SUB
    lane = lax.broadcasted_iota(jnp.int32, (SUB, TILE), 1)
    sub = lax.broadcasted_iota(jnp.int32, (SUB, TILE), 0)
    wide = (SUB, TILE)
    left = [block[SUB * g:SUB * (g + 1), :] for g in range(groups)]
    right = [(lane == sub + SUB * g).astype(jnp.float32) for g in range(groups)]
    for g in range(groups):
        base = SUB * g
        cols = [jnp.broadcast_to(left[g][:, base + t:base + t + 1], wide) for t in range(SUB)]
        pivots, invs, rows, rows_e = [], [], [], []
        for s in range(SUB):
            scal = [jnp.broadcast_to(cols[t][s:s + 1, :], wide) for t in range(s, SUB)]
            inv = 1.0 / scal[0]
            mult = jnp.where(sub > s, cols[s] * inv, 0.0)
            for t in range(s + 1, SUB):
                cols[t] = cols[t] - mult * scal[t - s]
            row = jnp.broadcast_to(left[g][s:s + 1, :], wide)
            row_e = jnp.broadcast_to(right[g][s:s + 1, :], wide)
            left[g] = left[g] - mult * row
            right[g] = right[g] - mult * row_e
            pivots.append(scal)
            invs.append(inv)
            rows.append(row)
            rows_e.append(row_e)
        for h in range(g + 1, groups):
            cols = [jnp.broadcast_to(left[h][:, base + t:base + t + 1], wide) for t in range(SUB)]
            for s in range(SUB):
                mult = cols[s] * invs[s]
                for t in range(s + 1, SUB):
                    cols[t] = cols[t] - mult * pivots[s][t - s]
                left[h] = left[h] - mult * rows[s]
                right[h] = right[h] - mult * rows_e[s]
    for g in range(groups):
        pivot = jnp.sum(jnp.where(lane == sub + SUB * g, left[g], 0.0), axis=1, keepdims=True)
        root = jnp.sqrt(pivot)
        left[g] = jnp.where(lane >= sub + SUB * g, left[g] / root, 0.0)
        right[g] = jnp.where(lane <= sub + SUB * g, right[g] / root, 0.0)
    return jnp.concatenate(left, axis=0), jnp.concatenate(right, axis=0)


def dot_tt(a, b):
    return lax.dot_general(a, b, (TT, ((), ())), preferred_element_type=jnp.float32)


def split2(x):
    hi = x.astype(jnp.bfloat16)
    return hi, (x - hi.astype(jnp.float32)).astype(jnp.bfloat16)


def dot_pairs(a, b, dims):
    def one(x, y):
        return lax.dot_general(x, y, (dims, ((), ())), preferred_element_type=jnp.float32)
    return one(a[0], b[0]) + (one(a[0], b[1]) + one(a[1], b[0]))


NN = ((1,), (0,))
TT = ((0,), (0,))


def eliminate(tiles, tri_ref, lift, inverse, high, low, ready, panel_ready):
    n = tiles * TILE

    def step(k, carry):
        here = pl.ds(pl.multiple_of(k * TILE, TILE), TILE)
        for kk in range(tiles):
            @pl.when(k == kk)
            def _(kk=kk):
                ready(kk)
                if kk:
                    at = kk * TILE
                    rows = slice(at, at + TILE)
                    own = (high[:at, rows], low[:at, rows])
                    change = dot_pairs(own, (high[:at, at:], low[:at, at:]), TT)
                    tri_ref[rows, at:] = tri_ref[rows, at:] - change[:, :n - at]
                    lift[rows, :] = lift[rows, :] - change[:, n - at:]

        upper, inv = factor_tile(tri_ref[here, here])
        inverse[here, :] = inv
        tri_ref[here, here] = upper
        for kk in range(tiles):
            @pl.when(k == kk)
            def _(kk=kk):
                panel_ready(kk)
                rows = slice(kk * TILE, (kk + 1) * TILE)
                right = (kk + 1) * TILE
                rest = jnp.concatenate([tri_ref[rows, right:], lift[rows, :]], axis=1) if right < n else lift[rows, :]
                panel = dot_pairs(split2(inverse[rows, :]), split2(rest), NN)
                if right < n:
                    tri_ref[rows, right:] = panel[:, :n - right]
                lift[rows, :] = panel[:, n - right:]
                high[rows, right:], low[rows, right:] = split2(panel)
        return carry

    lax.fori_loop(0, tiles, step, 0)


def back_solve(tiles, lift, inverse, high, low, direction, dir_high, dir_low):
    n = tiles * TILE
    for k in range(tiles - 1, -1, -1):
        rows = slice(k * TILE, (k + 1) * TILE)
        right = (k + 1) * TILE
        rest = lift[rows, :]
        if right < n:
            rest = rest - dot_pairs((high[rows, right:n], low[rows, right:n]), (dir_high[right:, :], dir_low[right:, :]), NN)
        part = dot_pairs(split2(inverse[rows, :]), split2(rest), TT)
        direction[rows, :] = part
        dir_high[rows, :], dir_low[rows, :] = split2(part)


def tile_of(t, tiles):
    row, offset = 0, 0
    start = 0
    for r in range(1, tiles):
        start = start + tiles - r + 1
        past = (t - start + tiles * tiles) // (tiles * tiles)
        row = row + past
        offset = offset + past * (tiles - r + 1)
    return row, t - offset + row


def parity(value, bits):
    width = 1
    while width < bits:
        width *= 2
    while width > 1:
        width //= 2
        value = value ^ (value >> width)
    return value & 1


def bit_of(value, bit):
    return lax.rem(value // (1 << bit), 2)


def step_kernel(mat_hbm, signs_ref, picks_ref, rhs_ref, tri_ref, solution_ref, residual_ref,
                mat_ref, signed, dense, picks_out, picks_all, table, mixed_high, mixed_low, partial, landed, sketch,
                atb_send, atb_land, sums, arrived, gathered, lift, inverse, high, low, mat_high, mat_low,
                direction, dir_high, dir_low, squares, gamma_out, gamma_all,
                mat_sem, send_sem, recv_sem, layer_sem, same_sem, sum_sem, tile_sem, pair_sem):
    devices = picks_all.shape[0]
    tiles, rows, _ = dense.shape
    planes, depth, _ = partial.shape
    stages = planes.bit_length() - 1
    slots = gathered.shape[1] - 1
    n = tiles * TILE
    samp = depth // tiles
    per = TILE // samp
    me = place()
    z, q = me // tiles, lax.rem(me, tiles)
    base = z * tiles
    partner = base + q + 1 - 2 * lax.rem(q, 2)
    family = [lax.rem(q + 2 * d, tiles) for d in range(1, tiles // 2)]
    across = [(z + (1 - 2 * bit_of(z, b)) * (1 << b)) * tiles + q for b in range(stages)]
    scale = 1.0 / math.sqrt(samp * devices)
    height = [TILE] * slots + [TILE + SUB]

    fetch = pltpu.make_async_copy(mat_hbm, mat_ref, mat_sem)
    fetch.start()
    barrier = greet(devices, me)
    own_picks = jnp.concatenate([picks_ref[...]] * per, axis=1)
    picks_out[...] = own_picks
    picks_all[me] = own_picks
    bands = rows // TILE
    sign_rows = jnp.concatenate([signs_ref[...].astype(jnp.float32)] * (SUB // bands), axis=0)
    sign = jnp.transpose(sign_rows)
    fetch.wait()
    for b in range(bands):
        band = slice(b * TILE, (b + 1) * TILE)
        flip = jnp.broadcast_to(sign[:, b:b + 1], (TILE, TILE))
        for p in range(tiles):
            signed[p, band, :] = mat_ref[band, p * TILE:(p + 1) * TILE] * flip
    pl.semaphore_wait(barrier, devices - 1)

    def send_picks(d):
        send(picks_out, picks_all.at[me], send_sem.at[0], recv_sem.at[0], lax.rem(me + d, devices))

    loop(1, devices, send_picks)

    def send_dense(d):
        p = lax.rem(q + d, tiles)
        send(signed.at[p], dense.at[q], send_sem.at[1], recv_sem.at[1], base + p)

    loop(1, tiles, send_dense)
    dense[q] = signed[q]

    rhs = rhs_ref[...]
    rhs_pair = split2(rhs)
    part_squares = jnp.broadcast_to(jnp.sum(rhs * rhs, axis=0, keepdims=True), (SUB, TILE))
    mat_high[...], mat_low[...] = split2(mat_ref[...])

    def atb_tile(p):
        here = pl.ds(pl.multiple_of(p * TILE, TILE), TILE)
        atb_send[p, :TILE, :] = dot_pairs((mat_high[:, here], mat_low[:, here]), rhs_pair, TT)
        atb_send[p, TILE:, :] = part_squares

    loop(0, tiles, atb_tile)
    atb_land[q] = atb_send[q]

    for i in range(1, tiles):
        tri_ref[i * TILE:(i + 1) * TILE, :i * TILE] = jnp.zeros((TILE, i * TILE), jnp.float32)

    await_bytes(picks_all.at[pl.ds(0, devices - 1)], recv_sem.at[0])
    lane = lax.broadcasted_iota(jnp.int32, (1, TILE), 1)

    def table_of(group, qk):
        row = picks_all[group * per * tiles + qk]
        for e in range(1, per):
            row = jnp.where(lane >= e * samp, picks_all[(group * per + e) * tiles + qk], row)
        counter = lax.broadcasted_iota(jnp.int32, (rows, TILE), 0)
        odd = parity(counter & row, (rows - 1).bit_length())
        return (1 - 2 * odd).astype(jnp.float32).astype(jnp.bfloat16)

    kept = table.shape[0] > 1
    if kept:
        def fill_table(c):
            table[c] = table_of(c // tiles, lax.rem(c, tiles))

        loop(0, planes // per * tiles, fill_table)

    await_bytes(dense.at[pl.ds(0, tiles - 1)], recv_sem.at[1])

    def send_atb(d):
        p = lax.rem(q + d, tiles)
        send(atb_send.at[p], atb_land.at[q], send_sem.at[2], recv_sem.at[2], base + p)

    loop(1, tiles, send_atb)
    chunk = 32

    def butterfly(c):
        here = pl.ds(pl.multiple_of(c * chunk, chunk), chunk)
        parts = [dense[d, here, :] for d in range(tiles)]
        span = 1
        while span < tiles:
            parts = [parts[d] + parts[d + span] if d // span % 2 == 0 else parts[d - span] - parts[d]
                     for d in range(tiles)]
            span *= 2
        for d in range(tiles):
            mixed_high[d, here, :], mixed_low[d, here, :] = split2(parts[d])

    loop(0, rows // chunk, butterfly)

    sizes = [planes >> (b + 1) for b in range(stages)]
    starts = [0]
    for b in range(stages):
        starts.append(starts[b] + bit_of(z, b) * sizes[b])
    landing = [sum(sizes[:b]) for b in range(stages)]

    def send_layer(b, here, sem):
        away = starts[b] + (1 - bit_of(z, b)) * sizes[b]
        send(partial.at[pl.ds(away, sizes[b]), here], landed.at[pl.ds(landing[b], sizes[b]), here],
             send_sem.at[3], sem, across[b])

    def project(qk):
        here = pl.ds(pl.multiple_of(qk * samp, samp), samp)
        for group in range(planes // per):
            rows_of = table[group * tiles + qk] if kept else table_of(group, qk)
            block = dot_tt(rows_of, mixed_high[qk]) + dot_tt(rows_of, mixed_low[qk])
            for e in range(per):
                zk = group * per + e
                slot = sum((zk >> b & 1) * sizes[b] for b in range(stages))
                odd = jnp.int32(0)
                for b in range(stages):
                    if zk >> b & 1:
                        odd = odd + bit_of(z, b)
                flip = 1.0 - 2.0 * lax.rem(odd, 2).astype(jnp.float32)
                partial[slot, here, :] = block[e * samp:(e + 1) * samp, :] * (flip * scale)
        send_layer(0, here, layer_sem.at[0, qk])

    loop(0, tiles, project)

    def combine(b, qk):
        here = slice(qk * samp, (qk + 1) * samp)
        await_bytes(landed.at[pl.ds(landing[b], sizes[b]), here], layer_sem.at[b, qk])
        total = partial[pl.ds(starts[b + 1], sizes[b]), here, :] + landed[pl.ds(landing[b], sizes[b]), here, :]
        if b + 1 < stages:
            partial[pl.ds(starts[b + 1], sizes[b]), here, :] = total
            send_layer(b + 1, here, layer_sem.at[b + 1, qk])
            return
        sketch[q, here, :] = total[0]
        mine = sketch.at[q, here]
        for p in family:
            send(mine, mine, send_sem.at[4], same_sem.at[qk], base + p)
        send(mine, mine, send_sem.at[5], recv_sem.at[3], partner)

    def relay(qk):
        here = slice(qk * samp, (qk + 1) * samp)
        await_bytes(sketch.at[pl.ds(0, len(family)), here], same_sem.at[qk])
        for p in family:
            send(sketch.at[p, here], sketch.at[p, here], send_sem.at[5], recv_sem.at[3], partner)

    lag = 2
    for t in range(tiles + lag * stages):
        for b in range(stages):
            if 0 <= t - lag * b < tiles:
                combine(b, t - lag * b)
        if 0 <= t - lag * stages < tiles:
            relay(t - lag * stages)

    await_bytes(atb_land.at[pl.ds(0, tiles - 1)], recv_sem.at[2])
    sums[0, slots] = jnp.sum(atb_land[...], axis=0)

    def send_sum(b, s):
        send(sums.at[b, s, :height[s]], arrived.at[b, s, :height[s]], send_sem.at[6], sum_sem.at[b, s], across[b])

    await_bytes(sketch.at[pl.ds(0, tiles // 2)], recv_sem.at[3])
    order = [0, slots] + list(range(1, slots))
    for s in order:
        if s < slots:
            t = jnp.minimum(s * tiles + q, tiles * (tiles + 1) // 2 - 1)
            i, j = tile_of(t, tiles)
            sums[0, s, :TILE, :] = dot_pairs(split2(sketch[i]), split2(sketch[j]), TT)
        send_sum(0, s)

    done = set()

    def once(name, s):
        fresh = (name, s) not in done
        done.add((name, s))
        return fresh

    def add_up(b, s):
        if not once(b, s):
            return
        if b:
            add_up(b - 1, s)
        await_bytes(arrived.at[b, s, :height[s]], sum_sem.at[b, s])
        total = sums[b, s, :height[s], :] + arrived[b, s, :height[s], :]
        if b + 1 < stages:
            sums[b + 1, s, :height[s], :] = total
            send_sum(b + 1, s)
            return
        gathered[q, s] = total[:TILE]
        if s == slots:
            squares[...] = total[TILE:]
        mine = gathered.at[q, s]
        for p in family:
            send(mine, mine, send_sem.at[7], tile_sem.at[s], base + p)
        send(mine, mine, send_sem.at[8], pair_sem.at[s], partner)

    def pass_on(s):
        if not once("pass", s):
            return
        add_up(stages - 1, s)
        await_bytes(gathered.at[pl.ds(0, len(family)), s], tile_sem.at[s])
        for p in family:
            send(gathered.at[p, s], gathered.at[p, s], send_sem.at[8], pair_sem.at[s], partner)

    def take(s):
        if not once("take", s):
            return
        pass_on(s)
        await_bytes(gathered.at[pl.ds(0, tiles // 2), s], pair_sem.at[s])
        for p in range(tiles):
            if s == slots:
                lift[p * TILE:(p + 1) * TILE, :] = gathered[p, s]
            elif s * tiles + p < tiles * (tiles + 1) // 2:
                i, j = tile_of(s * tiles + p, tiles)
                tri_ref[i * TILE:(i + 1) * TILE, j * TILE:(j + 1) * TILE] = gathered[p, s]

    last = [(sum(tiles - r for r in range(k + 1)) - 1) // tiles for k in range(tiles)]

    def ready(k):
        if k == 0:
            for b in range(stages - 1):
                for s in order:
                    add_up(b, s)
            for s in order[:3]:
                add_up(stages - 1, s)
            take(0)
            return
        if k + 2 < slots:
            add_up(stages - 1, k + 2)
        for s in range(last[k] + 1):
            take(s)
        if k + 1 < slots:
            pass_on(k + 1)

    def panel_ready(k):
        if k == 0:
            pass_on(slots)
            pass_on(1)
            add_up(stages - 1, 2)
            take(slots)

    eliminate(tiles, tri_ref, lift, inverse, high, low, ready, panel_ready)

    beta = jnp.sqrt(squares[0:1, :])
    lifted = lift[...] / beta
    alpha = jnp.sqrt(jnp.sum(lifted * lifted, axis=0, keepdims=True))
    lift[...] = lifted / alpha
    back_solve(tiles, lift, inverse, high, low, direction, dir_high, dir_low)

    rhs = rhs_ref[...]
    image = dot_pairs((mat_high[...], mat_low[...]), (dir_high[...], dir_low[...]), NN)
    pushed = image - alpha / beta * rhs
    gamma_out[...] = jnp.sum(pushed * pushed, axis=0, keepdims=True)
    gamma_all[me] = gamma_out[...]

    def send_gamma(d):
        send(gamma_out, gamma_all.at[me], send_sem.at[9], recv_sem.at[4], lax.rem(me + d, devices))

    loop(1, devices, send_gamma)

    def drain(d):
        await_bytes(picks_out, send_sem.at[0])

    loop(1, devices, drain)
    await_bytes(dense.at[pl.ds(0, tiles - 1)], send_sem.at[1])
    await_bytes(atb_land.at[pl.ds(0, tiles - 1)], send_sem.at[2])
    await_bytes(partial.at[pl.ds(0, planes - 1)], send_sem.at[3])
    await_bytes(sketch.at[pl.ds(0, len(family))], send_sem.at[4])
    await_bytes(sketch.at[pl.ds(0, tiles // 2)], send_sem.at[5])
    for s in range(slots + 1):
        for b in range(stages):
            await_bytes(arrived.at[b, s, :height[s]], send_sem.at[6])
        await_bytes(gathered.at[pl.ds(0, len(family)), s], send_sem.at[7])
        await_bytes(gathered.at[pl.ds(0, tiles // 2), s], send_sem.at[8])

    await_bytes(gamma_all.at[pl.ds(0, devices - 1)], recv_sem.at[4])
    gamma = jnp.sqrt(jnp.sum(gamma_all[...], axis=0))
    coef = beta * alpha / (alpha * alpha + gamma * gamma)
    solution_ref[...] = direction[...] * coef
    residual_ref[...] = rhs - image * coef
    await_bytes(gamma_all.at[pl.ds(0, devices - 1)], send_sem.at[9])


def shards(mat, signs, picks, rhs):
    devices = lax.axis_size("rows") * lax.axis_size("grp")
    rows, n = mat.shape
    tiles = n // TILE
    samp = picks.shape[0]
    planes = devices // tiles
    stages = planes.bit_length() - 1
    per = TILE // samp
    slots = (tiles * (tiles + 1) // 2 + tiles - 1) // tiles
    tables = planes // per * tiles
    if tables > 2 * tiles:
        tables = 1
    vmem = pl.BlockSpec(memory_space=pltpu.VMEM)
    f32, bf16, dma = jnp.float32, jnp.bfloat16, pltpu.SemaphoreType.DMA
    scratch = [
        ((rows, n), f32),
        ((tiles, rows, TILE), f32),
        ((tiles, rows, TILE), f32),
        ((1, TILE), jnp.int32),
        ((devices, 1, TILE), jnp.int32),
        ((tables, rows, TILE), bf16),
        ((tiles, rows, TILE), bf16),
        ((tiles, rows, TILE), bf16),
        ((planes, tiles * samp, TILE), f32),
        ((planes - 1, tiles * samp, TILE), f32),
        ((tiles, tiles * samp, TILE), f32),
        ((tiles, TILE + SUB, TILE), f32),
        ((tiles, TILE + SUB, TILE), f32),
        ((stages, slots + 1, TILE + SUB, TILE), f32),
        ((stages, slots + 1, TILE + SUB, TILE), f32),
        ((tiles, slots + 1, TILE, TILE), f32),
        ((n, TILE), f32),
        ((n, TILE), f32),
        ((n, n + TILE), bf16),
        ((n, n + TILE), bf16),
        ((rows, n), bf16),
        ((rows, n), bf16),
        ((n, TILE), f32),
        ((n, TILE), bf16),
        ((n, TILE), bf16),
        ((SUB, TILE), f32),
        ((1, TILE), f32),
        ((devices, 1, TILE), f32),
    ]
    return pl.pallas_call(
        step_kernel,
        out_shape=(
            jax.ShapeDtypeStruct((n, n), f32),
            jax.ShapeDtypeStruct((n, TILE), f32),
            jax.ShapeDtypeStruct((rows, TILE), f32),
        ),
        in_specs=[pl.BlockSpec(memory_space=pl.ANY)] + [vmem] * 3,
        out_specs=(vmem, vmem, vmem),
        scratch_shapes=[pltpu.VMEM(*entry) for entry in scratch] + [
            dma,
            dma((10,)),
            dma((5,)),
            dma((stages, tiles)),
            dma((tiles,)),
            dma((stages, slots + 1)),
            dma((slots + 1,)),
            dma((slots + 1,)),
        ],
        compiler_params=pltpu.CompilerParams(
            collective_id=0, has_side_effects=True, vmem_limit_bytes=(38 if tables > 1 else 56) * 1024 * 1024),
        name="sketch_solve",
    )(mat, signs.reshape(rows // TILE, TILE), picks.reshape(1, samp), rhs)


def solution(mesh):
    return jax.shard_map(
        shards,
        mesh=mesh,
        in_specs=(P(AXES, None), P(AXES), P(AXES), P(AXES, None)),
        out_specs=(P(), P(), P(AXES, None)),
        check_vma=False,
    )
```

time: 163 us -> 142 us (0.87)
  Pallas kernels: 153 us -> 134 us
    pallas_call x2 -> x1, Pallas kernels: 153 us -> 134 us  [shards(): pl.pallas_call(step_kernel, out_shape=(jax.ShapeDtypeStruct((n, n), f32),...]
    unnamed x7 -> x11, local copies, waits for them, and re-layouts: 6.36 us -> 7.38 us
where the time goes in v3:
time: 142 us
  Pallas kernels  134 us (94%)
  local copies, waits for them, and re-layouts  7.38 us (5%)
    pallas_call x1, Pallas kernels, shards(): pl.pallas_call(step_kernel, out_shape=(jax.ShapeDtypeStruct((n, n), f32),...  134 us
    unnamed x11, local copies, waits for them, and re-layouts  7.38 us

profile of v3, /device:TPU:0, one launch (start us, length us, event | category | flops | bytes accessed | tf_op | source)
XLA Modules:
  0.0 141.9 jit_solution(14603249171135736850)
XLA Ops:
  0.6 0.0 copy-start
  0.6 1.6 %copy-done = f32[512,1024]{1,0:T(8,128)S(1)} copy-done((f32[512,1024]{1,0:T(8,128)S(1)}, f32[512,1024]{1,0:T(8,128)}, u32[]{:S(2)}) %copy-start) | copy-done | bytes 2097176
  2.2 0.0 copy-start.1
  2.2 0.9 copy-done.1
  3.2 0.0 copy-start.2
  3.2 0.7 copy-done.2
  3.9 0.0 copy-start.3
  3.9 0.7 copy-done.3
  4.5 133.9 %sketch_solve.1 = (f32[1024,1024]{1,0:T(8,128)S(1)}, f32[1024,128]{1,0:T(8,128)S(1)}, f32[512,128]{1,0:T(8,128)S(1)}) custom-call(f32[512,1024]{1,0:T(8,128)S(1)} %copy-done, s32[4,128]{1,0:T(4,128)S(1)} %bitcast.2, s32[1,64]{1,0:T(1,128)S(1)} %bitcast.3, f32[512,128]{1,0:T(8,128)S(1)} %copy-done.1), custom_call_target="tpu_custom_call" | custom-call | tf_op jit(solution)/shard_map/sketch_solve/pallas_call | solution.py:526
  138.4 2.0 %copy.10 = f32[1024,1024]{1,0:T(8,128)} copy(f32[1024,1024]{1,0:T(8,128)S(1)} %get-tuple-element.6) | data formatting | bytes 8388608
  140.4 0.8 copy.11
  141.2 0.7 copy.12
Async XLA Ops:
  0.6 1.6 %copy-start = (f32[512,1024]{1,0:T(8,128)S(1)}, f32[512,1024]{1,0:T(8,128)}, u32[]{:S(2)}) copy-start(f32[512,1024]{1,0:T(8,128)} %mat_hbm.1) | copy-start | bytes 6291460
  2.2 0.9 copy-start.1
  3.2 0.7 copy-start.2
  3.9 0.7 copy-start.3
